TPU v7x, 512 devices: a whole 4x4x16 slice. The times are simulated.
512 devices in a mesh: mp: 2 (over y_hi), tok: 8 (over x, core), lat: 32 (over z, y_lo).
Axes of the slice: x: 4, y: 4 (y_hi: 2, y_lo: 2; y = y_hi * 2 + y_lo), z: 16, core: 2. Of those that a mesh axis runs over, the one named last changes fastest.
Arguments:
- inputs: bfloat16 [2, 384, 4608], P('mp', 'lat', 'tok'), may hold values from -6 to 6
- gate_w: bfloat16 [2, 4608, 18432], P('mp', 'tok', 'lat'), may hold values from -0.09375 to 0.09375
- up_w: bfloat16 [2, 4608, 18432], P('mp', 'tok', 'lat'), may hold values from -0.09375 to 0.09375
- down_w: bfloat16 [2, 18432, 4608], P('mp', 'lat', 'tok'), may hold values from -0.046875 to 0.046875
- enc_w: bfloat16 [2, 4608, 8192], P('mp', 'tok', 'lat'), may hold values from -0.0625 to 0.0625
- enc_bias: float32 [8192], P('lat'), may hold values from -3 to 3
- dec_w: bfloat16 [8192, 2, 4608], P('lat', 'mp', 'tok'), may hold values from -0.0625 to 0.0625
- dec_bias: float32 [2, 4608], P('mp', 'tok'), may hold values from -3 to 3
Outputs:
- recon_error: float32 [2, 384, 4608], P('mp', 'lat', 'tok')
- dec_grad: float32 [8192, 2, 4608], P('lat', 'mp', 'tok')
- latent_grad: float32 [384, 8192], P(None, 'lat')
All inputs are finite; a program needn't handle non-finite values.
Results may differ from a plain program's by a relative error of at most 0.009.
Values may be sent and summed in bfloat16 or wider, within the bound.
A program may use at most 64 MiB of HBM per device.

v0:
```python
import jax
import jax.numpy as jnp
from jax import lax
from jax.sharding import PartitionSpec as P


def contract_rows(left, right):
    return lax.dot_general(
        left, right, (((0,), (0,)), ((), ())), preferred_element_type=jnp.float32
    )


def contract_cols(left, right):
    return lax.dot_general(
        left, right, (((1,), (1,)), ((), ())), preferred_element_type=jnp.float32
    )


def body(inputs, gate_w, up_w, down_w, enc_w, enc_bias, dec_w, dec_bias):
    x_rows = inputs[0]
    gathered = lax.all_gather(x_rows, "lat", axis=0, tiled=True)
    gate_local = gate_w[0]
    up_local = up_w[0]
    width = gate_local.shape[1]
    block = gathered
    both = lax.psum_scatter(
        jnp.concatenate(
            [
                jnp.dot(block, gate_local, preferred_element_type=jnp.float32),
                jnp.dot(block, up_local, preferred_element_type=jnp.float32),
            ],
            axis=1,
        ),
        "tok",
        scatter_dimension=0,
        tiled=True,
    )
    hidden = (jax.nn.gelu(both[:, :width], approximate=True) * both[:, width:]).astype(jnp.bfloat16)
    hidden_all = lax.all_gather(hidden, "tok", axis=0, tiled=True)
    down_local = down_w[0]
    block = hidden_all
    acts = lax.psum_scatter(
        jnp.dot(block, down_local, preferred_element_type=jnp.float32),
        "lat",
        scatter_dimension=0,
        tiled=True,
    ).astype(jnp.bfloat16)
    acts_all = lax.all_gather(acts, "lat", axis=0, tiled=True)
    partial_pre = jnp.dot(acts_all, enc_w[0], preferred_element_type=jnp.float32)
    pre = lax.psum(partial_pre, ("mp", "tok"))
    codes = jnp.maximum(pre + enc_bias, 0.0).astype(jnp.bfloat16)
    decoder = dec_w[:, 0, :]
    bias_row = dec_bias[0]
    block = codes
    recon = lax.psum_scatter(
        jnp.dot(block, decoder, preferred_element_type=jnp.float32),
        "lat",
        scatter_dimension=0,
        tiled=True,
    )
    error = recon + bias_row - acts.astype(jnp.float32)
    error_all = lax.all_gather(error.astype(jnp.bfloat16), "lat", axis=0, tiled=True)
    decoder_grad = contract_rows(codes, error_all)
    latent_grad = lax.psum(contract_cols(error_all, decoder), ("mp", "tok"))
    return (error[None], decoder_grad[:, None, :], latent_grad)


def solution(mesh):
    in_specs = (
        P("mp", "lat", "tok"),
        P("mp", "tok", "lat"),
        P("mp", "tok", "lat"),
        P("mp", "lat", "tok"),
        P("mp", "tok", "lat"),
        P("lat"),
        P("lat", "mp", "tok"),
        P("mp", "tok"),
    )
    out_specs = (P("mp", "lat", "tok"), P("lat", "mp", "tok"), P(None, "lat"))
    return jax.shard_map(body, mesh=mesh, in_specs=in_specs, out_specs=out_specs, check_vma=False)
```

profile of v0, /device:TPU:1, one launch (start us, length us, event | category | flops | bytes accessed | tf_op | source)
XLA Modules:
  0.0 789.7 jit_solution(4947730989583786598)
XLA Ops:
  7.2 0.0 copy-start
  7.2 0.0 reduce-scatter.8.cloned.1.call-start
  7.2 0.8 copy.20
  8.0 61.9 %all-gather = bf16[1,384,576]{2,0,1:T(2,128)(2,1)S(1)} all-gather(bf16[1,12,576]{2,0,1:T(2,128)(2,1)S(1)} %copy.20), channel_id=2, replica_groups=mesh['mp'=2,'tok'=8,'lat'=32] {'lat'}, dimensions={1}, use_global_device_ids=true | all-gather | bytes 456192 | tf_op jit(solution)/shard_map/all_gather | solution.py:21
  70.0 0.7 copy.21
  70.6 0.6 fusion.4
  71.3 0.6 fusion.6
  71.9 0.1 pad_maximum_fusion
  72.1 2.0 copy.25
  74.0 0.0 reduce-scatter.8.cloned.1.call-update
  74.1 0.0 all-reduce.7.cloned.1.call-start
  74.1 47.7 %reduce-scatter.8.cloned.1.call-done = f32[48,1152]{1,0:T(8,128)} async-done(((f32[384,1152]{1,0:T(8,128)}), f32[48,1152]{1,0:T(8,128)}) %reduce-scatter.8.cloned.1.call-update) | async-done | bytes 221200 | tf_op jit(solution)/shard_map/reduce_scatter | solution.py:26
  121.8 1.1 fusion.24
  122.9 15.4 %all_gather.13 = bf16[384,576]{1,0:T(8,128)(2,1)S(1)} all-gather(bf16[48,576]{1,0:T(8,128)(2,1)S(1)} %fusion.24), channel_id=1, replica_groups=mesh['mp'=2,'tok'=8,'lat'=32] {'tok'}, dimensions={0}, use_global_device_ids=true | all-gather | bytes 497664 | tf_op jit(solution)/shard_map/all_gather | solution.py:39
  138.2 0.6 fusion.2
  138.8 0.0 copy-start.5
  138.8 59.0 %fusion = f32[16,576]{1,0:T(8,128)S(1)} fusion(f32[384,576]{1,0:T(8,128)S(1)} %fusion.2), kind=kCustom, calls=%all-reduce-scatter | all-reduce-scatter fusion | flops 294913 | bytes 923648
  197.9 1.7 collective-permute-start
  199.6 2.1 collective-permute-start.1
  201.7 6.0 collective-permute-start.7
  207.7 4.9 collective-permute-start.2
  212.7 4.9 collective-permute-start.3
  217.6 0.0 collective-permute-done.7
  217.6 2.1 collective-permute-start.4
  219.8 3.5 collective-permute-start.5
  223.2 0.0 collective-permute-done.1
  223.2 2.8 collective-permute-start.6
  226.1 1.3 dynamic-slice.6
  228.0 0.0 collective-permute-done.2
  228.0 0.0 collective-permute-done.4
  228.0 0.0 collective-permute-done.5
  228.1 1.3 concatenate.4
  229.4 0.0 copy-start.2
  229.4 0.0 copy-start.6
  229.4 49.4 %all-gather.1 = bf16[32,12,576]{2,1,0:T(8,128)(2,1)S(1)} all-gather(bf16[1,12,576]{2,1,0:T(8,128)(2,1)S(1)} %fusion.31), channel_id=1, replica_groups=mesh['mp'=2,'tok'=8,'lat'=32] {'lat'}, dimensions={0}, use_global_device_ids=true | all-gather | bytes 456192 | tf_op jit(solution)/shard_map/all_gather | solution.py:48
  278.8 0.2 reshape.9
  279.1 1.1 fusion.14
  280.2 0.0 all-reduce.7.cloned.1.call-update
  280.2 0.0 all-reduce.9.cloned.1.call-start
  280.2 180.0 %all-reduce.7.cloned.1.call-done = f32[384,256]{1,0:T(8,128)} async-done(((f32[384,256]{1,0:T(8,128)}), f32[384,256]{1,0:T(8,128)}) %all-reduce.7.cloned.1.call-update) | async-done | bytes 393232 | tf_op jit(solution)/shard_map/psum | solution.py:50
  460.2 1.3 fusion.12
  461.6 59.2 %fusion.1 = f32[16,576]{1,0:T(8,128)S(1)} fusion(f32[384,576]{1,0:T(8,128)S(1)} %fusion.12), kind=kCustom, calls=%all-reduce-scatter.1 | all-reduce-scatter fusion | flops 294913 | bytes 923648
  520.7 1.3 collective-permute-start.10
  522.0 3.4 collective-permute-start.11
  525.5 7.0 collective-permute-start.15
  532.6 4.5 collective-permute-start.12
  537.1 3.9 collective-permute-start.13
  541.0 0.0 collective-permute-done.15
  541.0 2.9 collective-permute-start.14
  543.9 0.0 collective-permute-done.10
  543.9 3.1 collective-permute-start.8
  547.0 2.2 collective-permute-start.9
  549.2 0.0 collective-permute-done.12
  549.3 0.0 collective-permute-done.14
  549.3 1.0 collective-permute-done.9
  550.3 1.0 concatenate.5
  551.3 48.9 %all-gather.2 = bf16[32,12,576]{2,1,0:T(8,128)(2,1)S(1)} all-gather(bf16[1,12,576]{2,1,0:T(8,128)(2,1)S(1)} %get-tuple-element.18), channel_id=1, replica_groups=mesh['mp'=2,'tok'=8,'lat'=32] {'lat'}, dimensions={0}, use_global_device_ids=true | all-gather | bytes 456192 | tf_op jit(solution)/shard_map/all_gather | solution.py:62
  600.2 0.2 reshape.11
  600.4 1.1 fusion.10
  601.5 0.0 all-reduce.9.cloned.1.call-update
  601.5 0.6 copy.24
  602.2 1.2 convolution_bitcast_fusion
  603.3 178.1 %all-reduce.9.cloned.1.call-done = f32[384,256]{1,0:T(8,128)} async-done(((f32[384,256]{1,0:T(8,128)}), f32[384,256]{1,0:T(8,128)}) %all-reduce.9.cloned.1.call-update) | async-done | bytes 393232 | tf_op jit(solution)/shard_map/psum | solution.py:64
  781.4 1.8 copy.29
  (24 shorter events, 0.1 us)
Async XLA Ops:
  7.2 63.5 %copy-start = (bf16[1,576,576]{2,1,0:T(8,128)(2,1)S(1)}, bf16[1,576,576]{2,1,0:T(8,128)(2,1)}, u32[]{:S(2)}) copy-start(bf16[1,576,576]{2,1,0:T(8,128)(2,1)} %param.10) | copy-start | bytes 1990660
  7.2 114.6 %reduce-scatter.8.cloned.1.call-start = ((), (), s32[]{:S(2)}) async-start(), calls=%async_computation.3 | async-start | bytes 1990656 | tf_op jit(solution)/shard_map/reduce_scatter | solution.py:26
  70.0 1.3 copy-start.3
  74.0 64.2 %copy-start.4 = (bf16[1,576,576]{2,1,0:T(8,128)(2,1)S(1)}, bf16[1,576,576]{2,1,0:T(8,128)(2,1)}, u32[]{:S(2)}) copy-start(bf16[1,576,576]{2,1,0:T(8,128)(2,1)} %param.11) | copy-start | bytes 1990660
  74.1 386.2 %all-reduce.7.cloned.1.call-start = ((), (), s32[]{:S(2)}) async-start(), calls=%async_computation.1 | async-start | bytes 786432 | tf_op jit(solution)/shard_map/psum | solution.py:50
  138.8 140.3 %copy-start.5 = (bf16[1,576,256]{2,1,0:T(8,128)(2,1)S(1)}, bf16[1,576,256]{2,1,0:T(8,128)(2,1)}, u32[]{:S(2)}) copy-start(bf16[1,576,256]{2,1,0:T(8,128)(2,1)} %param.12) | copy-start | bytes 884740
  197.9 21.9 %collective-permute-start = (bf16[16,576]{1,0:T(8,128)(2,1)S(1)}, bf16[16,576]{1,0:T(8,128)(2,1)S(1)}, u32[]{:S(2)}, u32[]{:S(2)}) collective-permute-start(bf16[16,576]{1,0:T(8,128)(2,1)S(1)} %convert.14), channel_id=1, source_target_pairs={{0,1},{1,2},{2,3},{3,4},{4,5},{5,6},{6,7},{7,8},{8,9},{9,10},{10,1... | collective-permute-start | bytes 55304
  199.6 23.6 %collective-permute-start.1 = (bf16[16,576]{1,0:T(8,128)(2,1)S(1)}, bf16[16,576]{1,0:T(8,128)(2,1)S(1)}, u32[]{:S(2)}, u32[]{:S(2)}) collective-permute-start(bf16[16,576]{1,0:T(8,128)(2,1)S(1)} %convert.14), channel_id=1, source_target_pairs={{0,2},{1,3},{2,4},{3,5},{4,6},{5,7},{6,8},{7,9},{8,10},{9,11},{10,... | collective-permute-start | bytes 55304
  201.7 15.9 %collective-permute-start.7 = (bf16[12,576]{1,0:T(8,128)(2,1)S(1)}, bf16[12,576]{1,0:T(8,128)(2,1)S(1)}, u32[]{:S(2)}, u32[]{:S(2)}) collective-permute-start(bf16[12,576]{1,0:T(8,128)(2,1)S(1)} %slice.10), channel_id=1, source_target_pairs={{0,8},{1,9},{2,10},{3,11},{4,12},{5,13},{6,14},{7,15},{8,16},{9,17... | collective-permute-start | bytes 41480
  207.7 20.3 %collective-permute-start.2 = (bf16[16,576]{1,0:T(8,128)(2,1)S(1)}, bf16[16,576]{1,0:T(8,128)(2,1)S(1)}, u32[]{:S(2)}, u32[]{:S(2)}) collective-permute-start(bf16[16,576]{1,0:T(8,128)(2,1)S(1)} %convert.14), channel_id=1, source_target_pairs={{0,3},{1,4},{2,5},{3,6},{4,7},{5,8},{6,9},{7,10},{8,11},{9,12},{10... | collective-permute-start | bytes 55304
  212.7 15.3 %collective-permute-start.3 = (bf16[16,576]{1,0:T(8,128)(2,1)S(1)}, bf16[16,576]{1,0:T(8,128)(2,1)S(1)}, u32[]{:S(2)}, u32[]{:S(2)}) collective-permute-start(bf16[16,576]{1,0:T(8,128)(2,1)S(1)} %convert.14), channel_id=1, source_target_pairs={{0,4},{1,5},{2,6},{3,7},{4,8},{5,9},{6,10},{7,11},{8,12},{9,13},{1... | collective-permute-start | bytes 55304
  217.6 10.4 %collective-permute-start.4 = (bf16[16,576]{1,0:T(8,128)(2,1)S(1)}, bf16[16,576]{1,0:T(8,128)(2,1)S(1)}, u32[]{:S(2)}, u32[]{:S(2)}) collective-permute-start(bf16[16,576]{1,0:T(8,128)(2,1)S(1)} %convert.14), channel_id=1, source_target_pairs={{0,5},{1,6},{2,7},{3,8},{4,9},{5,10},{6,11},{7,12},{8,13},{9,14},{... | collective-permute-start | bytes 55304
  219.8 8.3 %collective-permute-start.5 = (bf16[16,576]{1,0:T(8,128)(2,1)S(1)}, bf16[16,576]{1,0:T(8,128)(2,1)S(1)}, u32[]{:S(2)}, u32[]{:S(2)}) collective-permute-start(bf16[16,576]{1,0:T(8,128)(2,1)S(1)} %convert.14), channel_id=1, source_target_pairs={{0,6},{1,7},{2,8},{3,9},{4,10},{5,11},{6,12},{7,13},{8,14},{9,15},... | collective-permute-start | bytes 55304
  223.2 4.8 collective-permute-start.6
  229.4 230.8 %copy-start.2 = (bf16[256,1,576]{0,2,1:T(8,128)(2,1)S(1)}, bf16[256,1,576]{0,2,1:T(8,128)(2,1)}, u32[]{:S(2)}) copy-start(bf16[256,1,576]{0,2,1:T(8,128)(2,1)} %param.14) | copy-start | bytes 884740
  229.4 230.8 %copy-start.6 = (f32[256]{0:T(256)S(1)}, f32[256]{0:T(256)}, u32[]{:S(2)}) copy-start(f32[256]{0:T(256)} %param.13) | copy-start | bytes 3076
  280.2 269.0 %copy-start.7 = (f32[1,576]{1,0:T(1,128)S(1)}, f32[1,576]{1,0:T(1,128)}, u32[]{:S(2)}) copy-start(f32[1,576]{1,0:T(1,128)} %param.15) | copy-start | bytes 6916
  280.2 501.2 %all-reduce.9.cloned.1.call-start = ((), (), s32[]{:S(2)}) async-start(), calls=%async_computation.2 | async-start | bytes 786432 | tf_op jit(solution)/shard_map/psum | solution.py:64
  520.7 23.1 %collective-permute-start.10 = (f32[16,576]{1,0:T(8,128)S(1)}, f32[16,576]{1,0:T(8,128)S(1)}, u32[]{:S(2)}, u32[]{:S(2)}) collective-permute-start(f32[16,576]{1,0:T(8,128)S(1)} %fusion.1), channel_id=1, source_target_pairs={{0,3},{1,4},{2,5},{3,6},{4,7},{5,8},{6,9},{7,10},{8,11},{9,12},{10... | collective-permute-start | bytes 110600
  522.0 24.9 %collective-permute-start.11 = (f32[16,576]{1,0:T(8,128)S(1)}, f32[16,576]{1,0:T(8,128)S(1)}, u32[]{:S(2)}, u32[]{:S(2)}) collective-permute-start(f32[16,576]{1,0:T(8,128)S(1)} %fusion.1), channel_id=1, source_target_pairs={{0,4},{1,5},{2,6},{3,7},{4,8},{5,9},{6,10},{7,11},{8,12},{9,13},{1... | collective-permute-start | bytes 110600
  525.5 15.5 %collective-permute-start.15 = (f32[12,576]{1,0:T(8,128)S(1)}, f32[12,576]{1,0:T(8,128)S(1)}, u32[]{:S(2)}, u32[]{:S(2)}) collective-permute-start(f32[12,576]{1,0:T(8,128)S(1)} %slice.11), channel_id=1, source_target_pairs={{0,8},{1,9},{2,10},{3,11},{4,12},{5,13},{6,14},{7,15},{8,16},{9,17... | collective-permute-start | bytes 82952
  532.6 16.7 %collective-permute-start.12 = (f32[16,576]{1,0:T(8,128)S(1)}, f32[16,576]{1,0:T(8,128)S(1)}, u32[]{:S(2)}, u32[]{:S(2)}) collective-permute-start(f32[16,576]{1,0:T(8,128)S(1)} %fusion.1), channel_id=1, source_target_pairs={{0,5},{1,6},{2,7},{3,8},{4,9},{5,10},{6,11},{7,12},{8,13},{9,14},{... | collective-permute-start | bytes 110600
  537.1 12.2 %collective-permute-start.13 = (f32[16,576]{1,0:T(8,128)S(1)}, f32[16,576]{1,0:T(8,128)S(1)}, u32[]{:S(2)}, u32[]{:S(2)}) collective-permute-start(f32[16,576]{1,0:T(8,128)S(1)} %fusion.1), channel_id=1, source_target_pairs={{0,6},{1,7},{2,8},{3,9},{4,10},{5,11},{6,12},{7,13},{8,14},{9,15},... | collective-permute-start | bytes 110600
  541.0 8.2 %collective-permute-start.14 = (f32[16,576]{1,0:T(8,128)S(1)}, f32[16,576]{1,0:T(8,128)S(1)}, u32[]{:S(2)}, u32[]{:S(2)}) collective-permute-start(f32[16,576]{1,0:T(8,128)S(1)} %fusion.1), channel_id=1, source_target_pairs={{0,7},{1,8},{2,9},{3,10},{4,11},{5,12},{6,13},{7,14},{8,15},{9,16}... | collective-permute-start | bytes 110600
  543.9 5.4 collective-permute-start.8
  547.0 3.3 collective-permute-start.9
  551.3 50.8 %copy-start.1 = (f32[384,256]{1,0:T(8,128)S(1)}, f32[384,256]{1,0:T(8,128)}, u32[]{:S(2)}) copy-start(f32[384,256]{1,0:T(8,128)} %all-reduce.7.cloned.1.call-done) | copy-start | bytes 1179652
Sparse Core Ops, SparseCore 0:
  74.2 47.5 reduce-scatter.7
  280.3 179.8 all-reduce.6
  601.6 179.7 all-reduce.8
where the time goes:
time: 790 us
  waiting for transfers between devices  407 us (52%)
  blocking collectives  294 us (37%)
  starting transfers between devices  56.6 us (7%)
  between operations  14.9 us (2%)
  local copies, waits for them, and re-layouts  10 us (1%)
    psum x1, waiting for transfers between devices, body(): pre = lax.psum(partial_pre, ('mp', 'tok'))  180 us
    psum x1, waiting for transfers between devices, body(): latent_grad = lax.psum(contract_cols(error_all, decoder), ('mp', 'tok'))  178 us
    unnamed x2, blocking collectives  118 us
    all_gather x1, blocking collectives, body(): gathered = lax.all_gather(x_rows, 'lat', axis=0, tiled=True)  61.9 us
    unnamed x16, starting transfers between devices  56.5 us
    all_gather x1, blocking collectives, body(): acts_all = lax.all_gather(acts, 'lat', axis=0, tiled=True)  49.4 us
    all_gather x1, blocking collectives, body(): lax.all_gather(error.astype(jnp.bfloat16), 'lat', axis=0, tiled=True)  48.9 us
    reduce_scatter x1, waiting for transfers between devices, body(): lax.psum_scatter(jnp.concatenate([jnp.dot(block, gate_local, preferred_el...  47.7 us
  transfers between devices with their start and end apart: 19, of which 4 were waited for; matrix products, arithmetic and copies ran while one was open for 0% of the time, Pallas kernels for 0%

commit v1 on v0

--- a/solution.py
+++ b/solution.py
@@ -59,7 +59,10 @@
         tiled=True,
     )
     error = recon + bias_row - acts.astype(jnp.float32)
-    error_all = lax.all_gather(error.astype(jnp.bfloat16), "lat", axis=0, tiled=True)
+    error_all = jnp.concatenate(
+        lax.all_to_all(jnp.stack([error.astype(jnp.bfloat16)] * lax.axis_size("lat")), "lat", 0, 0),
+        axis=0,
+    )
     decoder_grad = contract_rows(codes, error_all)
     latent_grad = lax.psum(contract_cols(error_all, decoder), ("mp", "tok"))
     return (error[None], decoder_grad[:, None, :], latent_grad)

time: 790 us -> 759 us (0.961)
  blocking collectives: 294 us -> 277 us
  waiting for transfers between devices: 407 us -> 392 us
    all_gather x1 -> x0, blocking collectives: 48.9 us -> none  [body(): lax.all_gather(error.astype(jnp.bfloat16), 'lat', axis=0, tiled=True)]
    all_to_all x0 -> x1, blocking collectives: none -> 32.4 us  [body(): lax.all_to_all(jnp.stack([error.astype(jnp.bfloat16)] * lax.axis_size('la...]
    psum x1, waiting for transfers between devices: 178 us -> 163 us  [body(): latent_grad = lax.psum(contract_cols(error_all, decoder), ('mp', 'tok'))]
where the time goes in v1:
time: 759 us; the launch traced here: 758 us
  waiting for transfers between devices  392 us (52%)
  blocking collectives  277 us (36%)
  starting transfers between devices  56.6 us (7%)
  between operations  14.9 us (2%)
  local copies, waits for them, and re-layouts  10.1 us (1%)
    psum x1, waiting for transfers between devices, body(): pre = lax.psum(partial_pre, ('mp', 'tok'))  180 us
    psum x1, waiting for transfers between devices, body(): latent_grad = lax.psum(contract_cols(error_all, decoder), ('mp', 'tok'))  163 us
    unnamed x2, blocking collectives  118 us
    all_gather x1, blocking collectives, body(): gathered = lax.all_gather(x_rows, 'lat', axis=0, tiled=True)  61.9 us
    unnamed x16, starting transfers between devices  56.5 us
    all_gather x1, blocking collectives, body(): acts_all = lax.all_gather(acts, 'lat', axis=0, tiled=True)  49.4 us
    reduce_scatter x1, waiting for transfers between devices, body(): lax.psum_scatter(jnp.concatenate([jnp.dot(block, gate_local, preferred_el...  47.7 us
    all_to_all x1, blocking collectives, body(): lax.all_to_all(jnp.stack([error.astype(jnp.bfloat16)] * lax.axis_size('la...  32.4 us
  transfers between devices with their start and end apart: 19, of which 4 were waited for; matrix products, arithmetic and copies ran while one was open for 0% of the time, Pallas kernels for 0%

profile of v1, /device:TPU:1, one launch (start us, length us, event | category | flops | bytes accessed | tf_op | source)
XLA Modules:
  0.0 758.1 jit_solution(1334212710827914043)
XLA Ops:
  7.2 0.0 copy-start
  7.2 0.0 reduce-scatter.8.cloned.1.call-start
  7.2 0.8 copy.20
  8.0 61.9 %all-gather = bf16[1,384,576]{2,0,1:T(2,128)(2,1)S(1)} all-gather(bf16[1,12,576]{2,0,1:T(2,128)(2,1)S(1)} %copy.20), channel_id=2, replica_groups=mesh['mp'=2,'tok'=8,'lat'=32] {'lat'}, dimensions={1}, use_global_device_ids=true | all-gather | bytes 456192 | tf_op jit(solution)/shard_map/all_gather | solution.py:21
  70.0 0.7 copy.21
  70.6 0.6 fusion.4
  71.3 0.6 fusion.6
  71.9 0.1 pad_maximum_fusion
  72.1 2.0 copy.25
  74.0 0.0 reduce-scatter.8.cloned.1.call-update
  74.1 0.0 all-reduce.7.cloned.1.call-start
  74.1 47.7 %reduce-scatter.8.cloned.1.call-done = f32[48,1152]{1,0:T(8,128)} async-done(((f32[384,1152]{1,0:T(8,128)}), f32[48,1152]{1,0:T(8,128)}) %reduce-scatter.8.cloned.1.call-update) | async-done | bytes 221200 | tf_op jit(solution)/shard_map/reduce_scatter | solution.py:26
  121.8 1.1 fusion.24
  122.9 15.4 %all_gather.10 = bf16[384,576]{1,0:T(8,128)(2,1)S(1)} all-gather(bf16[48,576]{1,0:T(8,128)(2,1)S(1)} %fusion.24), channel_id=1, replica_groups=mesh['mp'=2,'tok'=8,'lat'=32] {'tok'}, dimensions={0}, use_global_device_ids=true | all-gather | bytes 497664 | tf_op jit(solution)/shard_map/all_gather | solution.py:39
  138.2 0.6 fusion.2
  138.8 0.0 copy-start.5
  138.8 59.0 %fusion = f32[16,576]{1,0:T(8,128)S(1)} fusion(f32[384,576]{1,0:T(8,128)S(1)} %fusion.2), kind=kCustom, calls=%all-reduce-scatter | all-reduce-scatter fusion | flops 294913 | bytes 923648
  197.9 1.7 collective-permute-start
  199.6 2.1 collective-permute-start.1
  201.7 6.0 collective-permute-start.7
  207.7 4.9 collective-permute-start.2
  212.7 4.9 collective-permute-start.3
  217.6 0.0 collective-permute-done.7
  217.6 2.1 collective-permute-start.4
  219.8 3.5 collective-permute-start.5
  223.2 0.0 collective-permute-done.1
  223.2 2.8 collective-permute-start.6
  226.1 1.3 dynamic-slice.6
  228.0 0.0 collective-permute-done.2
  228.0 0.0 collective-permute-done.4
  228.0 0.0 collective-permute-done.5
  228.1 1.3 concatenate.4
  229.4 0.0 copy-start.2
  229.4 0.0 copy-start.6
  229.4 49.4 %all-gather.1 = bf16[32,12,576]{2,1,0:T(8,128)(2,1)S(1)} all-gather(bf16[1,12,576]{2,1,0:T(8,128)(2,1)S(1)} %fusion.30), channel_id=1, replica_groups=mesh['mp'=2,'tok'=8,'lat'=32] {'lat'}, dimensions={0}, use_global_device_ids=true | all-gather | bytes 456192 | tf_op jit(solution)/shard_map/all_gather | solution.py:48
  278.8 0.2 reshape.15
  279.1 1.1 fusion.14
  280.2 0.0 all-reduce.7.cloned.1.call-update
  280.2 0.0 all-reduce.9.cloned.1.call-start
  280.2 180.0 %all-reduce.7.cloned.1.call-done = f32[384,256]{1,0:T(8,128)} async-done(((f32[384,256]{1,0:T(8,128)}), f32[384,256]{1,0:T(8,128)}) %all-reduce.7.cloned.1.call-update) | async-done | bytes 393232 | tf_op jit(solution)/shard_map/psum | solution.py:50
  460.2 1.3 fusion.12
  461.6 59.2 %fusion.1 = f32[16,576]{1,0:T(8,128)S(1)} fusion(f32[384,576]{1,0:T(8,128)S(1)} %fusion.12), kind=kCustom, calls=%all-reduce-scatter.1 | all-reduce-scatter fusion | flops 294913 | bytes 923648
  520.7 1.3 collective-permute-start.10
  522.0 3.4 collective-permute-start.11
  525.5 7.0 collective-permute-start.15
  532.6 4.5 collective-permute-start.12
  537.1 3.9 collective-permute-start.13
  541.0 0.0 collective-permute-done.15
  541.0 2.9 collective-permute-start.14
  543.9 0.0 collective-permute-done.10
  543.9 3.1 collective-permute-start.8
  547.0 2.2 collective-permute-start.9
  549.2 0.0 collective-permute-done.12
  549.3 1.0 collective-permute-done.9
  550.3 1.0 concatenate.5
  551.3 0.1 stack.2
  551.4 32.4 %all_to_all.5 = bf16[32,12,576]{2,1,0:T(8,128)(2,1)S(1)} all-to-all(bf16[32,12,576]{2,1,0:T(8,128)(2,1)S(1)} %stack.2), channel_id=1, replica_groups=mesh['mp'=2,'tok'=8,'lat'=32] {'lat'}, dimensions={0} | all-to-all | bytes 884736 | tf_op jit(solution)/shard_map/all_to_all | solution.py:63
  583.8 0.2 reshape.12
  584.0 1.1 fusion.10
  585.1 0.0 all-reduce.9.cloned.1.call-update
  585.1 0.6 copy.24
  585.8 1.2 convolution_bitcast_fusion
  586.9 162.8 %all-reduce.9.cloned.1.call-done = f32[384,256]{1,0:T(8,128)} async-done(((f32[384,256]{1,0:T(8,128)}), f32[384,256]{1,0:T(8,128)}) %all-reduce.9.cloned.1.call-update) | async-done | bytes 393232 | tf_op jit(solution)/shard_map/psum | solution.py:67
  749.8 1.8 copy.29
  (25 shorter events, 0.1 us)
Async XLA Ops:
  7.2 63.5 %copy-start = (bf16[1,576,576]{2,1,0:T(8,128)(2,1)S(1)}, bf16[1,576,576]{2,1,0:T(8,128)(2,1)}, u32[]{:S(2)}) copy-start(bf16[1,576,576]{2,1,0:T(8,128)(2,1)} %param.10) | copy-start | bytes 1990660
  7.2 114.6 %reduce-scatter.8.cloned.1.call-start = ((), (), s32[]{:S(2)}) async-start(), calls=%async_computation.4 | async-start | bytes 1990656 | tf_op jit(solution)/shard_map/reduce_scatter | solution.py:26
  70.0 1.3 copy-start.3
  74.0 64.2 %copy-start.4 = (bf16[1,576,576]{2,1,0:T(8,128)(2,1)S(1)}, bf16[1,576,576]{2,1,0:T(8,128)(2,1)}, u32[]{:S(2)}) copy-start(bf16[1,576,576]{2,1,0:T(8,128)(2,1)} %param.11) | copy-start | bytes 1990660
  74.1 386.2 %all-reduce.7.cloned.1.call-start = ((), (), s32[]{:S(2)}) async-start(), calls=%async_computation.2 | async-start | bytes 786432 | tf_op jit(solution)/shard_map/psum | solution.py:50
  138.8 140.3 %copy-start.5 = (bf16[1,576,256]{2,1,0:T(8,128)(2,1)S(1)}, bf16[1,576,256]{2,1,0:T(8,128)(2,1)}, u32[]{:S(2)}) copy-start(bf16[1,576,256]{2,1,0:T(8,128)(2,1)} %param.12) | copy-start | bytes 884740
  197.9 21.9 %collective-permute-start = (bf16[16,576]{1,0:T(8,128)(2,1)S(1)}, bf16[16,576]{1,0:T(8,128)(2,1)S(1)}, u32[]{:S(2)}, u32[]{:S(2)}) collective-permute-start(bf16[16,576]{1,0:T(8,128)(2,1)S(1)} %convert.14), channel_id=1, source_target_pairs={{0,1},{1,2},{2,3},{3,4},{4,5},{5,6},{6,7},{7,8},{8,9},{9,10},{10,1... | collective-permute-start | bytes 55304
  199.6 23.6 %collective-permute-start.1 = (bf16[16,576]{1,0:T(8,128)(2,1)S(1)}, bf16[16,576]{1,0:T(8,128)(2,1)S(1)}, u32[]{:S(2)}, u32[]{:S(2)}) collective-permute-start(bf16[16,576]{1,0:T(8,128)(2,1)S(1)} %convert.14), channel_id=1, source_target_pairs={{0,2},{1,3},{2,4},{3,5},{4,6},{5,7},{6,8},{7,9},{8,10},{9,11},{10,... | collective-permute-start | bytes 55304
  201.7 15.9 %collective-permute-start.7 = (bf16[12,576]{1,0:T(8,128)(2,1)S(1)}, bf16[12,576]{1,0:T(8,128)(2,1)S(1)}, u32[]{:S(2)}, u32[]{:S(2)}) collective-permute-start(bf16[12,576]{1,0:T(8,128)(2,1)S(1)} %slice.10), channel_id=1, source_target_pairs={{0,8},{1,9},{2,10},{3,11},{4,12},{5,13},{6,14},{7,15},{8,16},{9,17... | collective-permute-start | bytes 41480
  207.7 20.3 %collective-permute-start.2 = (bf16[16,576]{1,0:T(8,128)(2,1)S(1)}, bf16[16,576]{1,0:T(8,128)(2,1)S(1)}, u32[]{:S(2)}, u32[]{:S(2)}) collective-permute-start(bf16[16,576]{1,0:T(8,128)(2,1)S(1)} %convert.14), channel_id=1, source_target_pairs={{0,3},{1,4},{2,5},{3,6},{4,7},{5,8},{6,9},{7,10},{8,11},{9,12},{10... | collective-permute-start | bytes 55304
  212.7 15.3 %collective-permute-start.3 = (bf16[16,576]{1,0:T(8,128)(2,1)S(1)}, bf16[16,576]{1,0:T(8,128)(2,1)S(1)}, u32[]{:S(2)}, u32[]{:S(2)}) collective-permute-start(bf16[16,576]{1,0:T(8,128)(2,1)S(1)} %convert.14), channel_id=1, source_target_pairs={{0,4},{1,5},{2,6},{3,7},{4,8},{5,9},{6,10},{7,11},{8,12},{9,13},{1... | collective-permute-start | bytes 55304
  217.6 10.4 %collective-permute-start.4 = (bf16[16,576]{1,0:T(8,128)(2,1)S(1)}, bf16[16,576]{1,0:T(8,128)(2,1)S(1)}, u32[]{:S(2)}, u32[]{:S(2)}) collective-permute-start(bf16[16,576]{1,0:T(8,128)(2,1)S(1)} %convert.14), channel_id=1, source_target_pairs={{0,5},{1,6},{2,7},{3,8},{4,9},{5,10},{6,11},{7,12},{8,13},{9,14},{... | collective-permute-start | bytes 55304
  219.8 8.3 %collective-permute-start.5 = (bf16[16,576]{1,0:T(8,128)(2,1)S(1)}, bf16[16,576]{1,0:T(8,128)(2,1)S(1)}, u32[]{:S(2)}, u32[]{:S(2)}) collective-permute-start(bf16[16,576]{1,0:T(8,128)(2,1)S(1)} %convert.14), channel_id=1, source_target_pairs={{0,6},{1,7},{2,8},{3,9},{4,10},{5,11},{6,12},{7,13},{8,14},{9,15},... | collective-permute-start | bytes 55304
  223.2 4.8 collective-permute-start.6
  229.4 230.8 %copy-start.2 = (bf16[256,1,576]{0,2,1:T(8,128)(2,1)S(1)}, bf16[256,1,576]{0,2,1:T(8,128)(2,1)}, u32[]{:S(2)}) copy-start(bf16[256,1,576]{0,2,1:T(8,128)(2,1)} %param.14) | copy-start | bytes 884740
  229.4 230.8 %copy-start.6 = (f32[256]{0:T(256)S(1)}, f32[256]{0:T(256)}, u32[]{:S(2)}) copy-start(f32[256]{0:T(256)} %param.13) | copy-start | bytes 3076
  280.2 269.0 %copy-start.7 = (f32[1,576]{1,0:T(1,128)S(1)}, f32[1,576]{1,0:T(1,128)}, u32[]{:S(2)}) copy-start(f32[1,576]{1,0:T(1,128)} %param.15) | copy-start | bytes 6916
  280.2 469.6 %all-reduce.9.cloned.1.call-start = ((), (), s32[]{:S(2)}) async-start(), calls=%async_computation.3 | async-start | bytes 786432 | tf_op jit(solution)/shard_map/psum | solution.py:67
  520.7 23.1 %collective-permute-start.10 = (f32[16,576]{1,0:T(8,128)S(1)}, f32[16,576]{1,0:T(8,128)S(1)}, u32[]{:S(2)}, u32[]{:S(2)}) collective-permute-start(f32[16,576]{1,0:T(8,128)S(1)} %fusion.1), channel_id=1, source_target_pairs={{0,3},{1,4},{2,5},{3,6},{4,7},{5,8},{6,9},{7,10},{8,11},{9,12},{10... | collective-permute-start | bytes 110600
  522.0 24.9 %collective-permute-start.11 = (f32[16,576]{1,0:T(8,128)S(1)}, f32[16,576]{1,0:T(8,128)S(1)}, u32[]{:S(2)}, u32[]{:S(2)}) collective-permute-start(f32[16,576]{1,0:T(8,128)S(1)} %fusion.1), channel_id=1, source_target_pairs={{0,4},{1,5},{2,6},{3,7},{4,8},{5,9},{6,10},{7,11},{8,12},{9,13},{1... | collective-permute-start | bytes 110600
  525.5 15.5 %collective-permute-start.15 = (f32[12,576]{1,0:T(8,128)S(1)}, f32[12,576]{1,0:T(8,128)S(1)}, u32[]{:S(2)}, u32[]{:S(2)}) collective-permute-start(f32[12,576]{1,0:T(8,128)S(1)} %slice.11), channel_id=1, source_target_pairs={{0,8},{1,9},{2,10},{3,11},{4,12},{5,13},{6,14},{7,15},{8,16},{9,17... | collective-permute-start | bytes 82952
  532.6 16.7 %collective-permute-start.12 = (f32[16,576]{1,0:T(8,128)S(1)}, f32[16,576]{1,0:T(8,128)S(1)}, u32[]{:S(2)}, u32[]{:S(2)}) collective-permute-start(f32[16,576]{1,0:T(8,128)S(1)} %fusion.1), channel_id=1, source_target_pairs={{0,5},{1,6},{2,7},{3,8},{4,9},{5,10},{6,11},{7,12},{8,13},{9,14},{... | collective-permute-start | bytes 110600
  537.1 12.2 %collective-permute-start.13 = (f32[16,576]{1,0:T(8,128)S(1)}, f32[16,576]{1,0:T(8,128)S(1)}, u32[]{:S(2)}, u32[]{:S(2)}) collective-permute-start(f32[16,576]{1,0:T(8,128)S(1)} %fusion.1), channel_id=1, source_target_pairs={{0,6},{1,7},{2,8},{3,9},{4,10},{5,11},{6,12},{7,13},{8,14},{9,15},... | collective-permute-start | bytes 110600
  541.0 8.2 %collective-permute-start.14 = (f32[16,576]{1,0:T(8,128)S(1)}, f32[16,576]{1,0:T(8,128)S(1)}, u32[]{:S(2)}, u32[]{:S(2)}) collective-permute-start(f32[16,576]{1,0:T(8,128)S(1)} %fusion.1), channel_id=1, source_target_pairs={{0,7},{1,8},{2,9},{3,10},{4,11},{5,12},{6,13},{7,14},{8,15},{9,16}... | collective-permute-start | bytes 110600
  543.9 5.4 collective-permute-start.8
  547.0 3.3 collective-permute-start.9
  551.4 34.4 %copy-start.1 = (f32[384,256]{1,0:T(8,128)S(1)}, f32[384,256]{1,0:T(8,128)}, u32[]{:S(2)}) copy-start(f32[384,256]{1,0:T(8,128)} %all-reduce.7.cloned.1.call-done) | copy-start | bytes 1179652
Sparse Core Ops, SparseCore 0:
  74.2 47.5 reduce-scatter.7
  280.3 179.8 all-reduce.6
  585.2 164.4 all-reduce.8
